TPU v7x, 128 devices: a whole 4x4x4 slice. The times are simulated.
128 devices in a mesh: shot: 32 (over x_lo, z, y), freq: 4 (over x_hi, core).
Axes of the slice: x: 4 (x_hi: 2, x_lo: 2; x = x_hi * 2 + x_lo), y: 4, z: 4, core: 2. Of those that a mesh axis runs over, the one named last changes fastest.
Arguments:
- recorded: bfloat16 [2, 256, 2048, 512], P(None, 'freq', 'shot'), may hold values from -6 to 6
- rec_shot: int32 [2048, 512], P('shot'), may hold values from 0 to 2047
- owners: int32 [3], replicated, may hold values from 0 to 31, as said below
Outputs:
- primaries: bfloat16 [2048, 512, 512], P('shot', 'freq')
- filters: float32 [2048, 31], P('shot')
Inputs may be any that keep to these rules, and one draw needn't show every extreme that they name: The 3 owners are distinct; the first and the last index of the shot axis are always among them.
All inputs are finite; a program needn't handle non-finite values.
Results may differ from a plain program's by a relative error of at most 0.008.
Values may be sent and summed in bfloat16 or wider, within the bound.
A program may use at most 192 MiB of HBM per device.

v0:
```python
import math

import jax
import jax.numpy as jnp
from jax import lax
from jax.sharding import PartitionSpec as P

F = 256
TAPS = 31
STEPS = 3


REG = 2.0


def broadcast(value, axis, source):
    kept = jnp.where(lax.axis_index(axis) == source, value, 0).astype(value.dtype)
    return lax.psum(kept, axis)


def angles(freq_index, step_index, period):
    product_mod = jnp.mod(freq_index[:, None] * step_index[None, :], period)
    return product_mod.astype(jnp.float32) * (2.0 * math.pi / period)


def solve_filters(autocorr, crosscorr, tap_count, damping):
    half_taps = (tap_count - 1) // 2
    tap_index = jnp.arange(tap_count, dtype=jnp.int32)
    distance = jnp.abs(tap_index[:, None] - tap_index[None, :])
    normal = autocorr[:, distance] + damping * jnp.eye(tap_count, dtype=jnp.float32)[None, :, :]
    target = crosscorr + damping * (tap_index == half_taps).astype(jnp.float32)[None, :]
    factor = jnp.linalg.cholesky(normal)
    middle = lax.linalg.triangular_solve(factor, target[:, :, None], left_side=True, lower=True)
    solved = lax.linalg.triangular_solve(
        factor, middle, left_side=True, lower=True, transpose_a=True
    )
    return solved[:, :, 0]


def band_table(freq_index, freq_count):
    period = 2 * freq_count
    phase_angles = angles(freq_index, jnp.arange(period, dtype=jnp.int32), period)
    norm_factor = 1.0 / math.sqrt(freq_count)
    return jnp.stack(
        [jnp.cos(phase_angles) * norm_factor, -jnp.sin(phase_angles) * norm_factor]
    ).astype(jnp.bfloat16)


def fetch_owner(data_slab, owner):
    return broadcast(data_slab, "shot", owner)


def product_step(data_slab, rec_shot, owner, owner_block):
    shot_count = data_slab.shape[2]
    offset_index = rec_shot - owner * shot_count
    slot_keys = jnp.arange(shot_count, dtype=jnp.int32)
    one_hot = (offset_index[:, None, :] == slot_keys[None, :, None]).astype(jnp.bfloat16)
    coeffs = jnp.einsum(
        "cfsr,skr->cfsk", data_slab, one_hot, preferred_element_type=jnp.float32
    ).astype(jnp.bfloat16)
    left_real = jnp.concatenate([coeffs[0], -coeffs[1]], axis=2)
    left_imag = jnp.concatenate([coeffs[1], coeffs[0]], axis=2)
    stacked = jnp.stack([left_real, left_imag])
    right_side = jnp.concatenate([owner_block[0], owner_block[1]], axis=1)
    return jnp.einsum("cfsk,fkr->cfsr", stacked, right_side, preferred_element_type=jnp.float32)


def per_device(recorded, rec_shot, owners):
    band_count = recorded.shape[1]
    recv_count = recorded.shape[3]
    half_taps = (TAPS - 1) // 2
    summed = jnp.zeros(recorded.shape, jnp.float32)
    for step_index in range(STEPS):
        owner_block = fetch_owner(recorded, owners[step_index])
        summed = summed + product_step(recorded, rec_shot, owners[step_index], owner_block)
    pred_gain = (lax.axis_size("shot") / (2.0 * recv_count * STEPS)) ** 0.5
    predicted = (pred_gain * summed).astype(jnp.bfloat16)
    pred_wide = predicted.astype(jnp.float32)
    data_wide = recorded.astype(jnp.float32)
    spectrum = jnp.sum(pred_wide[0] * pred_wide[0] + pred_wide[1] * pred_wide[1], axis=2)
    cross_real = jnp.sum(pred_wide[0] * data_wide[0] + pred_wide[1] * data_wide[1], axis=2)
    cross_imag = jnp.sum(pred_wide[0] * data_wide[1] - pred_wide[1] * data_wide[0], axis=2)
    highest = lax.Precision.HIGHEST
    freq_index = lax.axis_index("freq") * band_count + jnp.arange(band_count, dtype=jnp.int32)
    tap_index = jnp.arange(TAPS, dtype=jnp.int32)
    lag_angles = angles(freq_index, tap_index, 2 * F)
    tap_angles = angles(freq_index, tap_index - half_taps, 2 * F)
    auto_part = jnp.dot(spectrum.T, jnp.cos(lag_angles), precision=highest)
    cross_part = jnp.dot(cross_real.T, jnp.cos(tap_angles), precision=highest) - jnp.dot(
        cross_imag.T, jnp.sin(tap_angles), precision=highest
    )
    autocorr, crosscorr = lax.psum((auto_part, cross_part), "freq")
    filters = solve_filters(autocorr, crosscorr, TAPS, REG * recv_count * F)
    resp_real = jnp.dot(jnp.cos(tap_angles), filters.T, precision=highest)[:, :, None]
    resp_imag = -jnp.dot(jnp.sin(tap_angles), filters.T, precision=highest)[:, :, None]
    res_real = data_wide[0] - (resp_real * pred_wide[0] - resp_imag * pred_wide[1])
    res_imag = data_wide[1] - (resp_real * pred_wide[1] + resp_imag * pred_wide[0])
    residual = jnp.stack([res_real, res_imag]).astype(jnp.bfloat16)
    full_table = band_table(jnp.arange(F, dtype=jnp.int32), F).reshape(2 * F, 2 * F)
    shard_piece = lax.all_to_all(residual, "freq", split_axis=3, concat_axis=1, tiled=True)
    item_count = shard_piece.shape[2]
    recv_part = shard_piece.shape[3]
    flattened = shard_piece.reshape(2 * F, item_count * recv_part)
    time_rows = lax.dot_general(
        flattened, full_table, (((0,), (0,)), ((), ())), preferred_element_type=jnp.float32
    )
    primaries = time_rows.reshape(item_count, recv_part, 2 * F).astype(jnp.bfloat16)
    return (primaries, filters)


def solution(mesh):
    placed = (P(None, "freq", "shot", None), P("shot", None), P())
    return jax.shard_map(
        per_device,
        mesh=mesh,
        in_specs=placed,
        out_specs=(P("shot", "freq", None), P("shot", None)),
        check_vma=False,
    )
```

profile of v0, /device:TPU:1, one launch (start us, length us, event | category | flops | bytes accessed | tf_op | source)
XLA Modules:
  0.0 1144.3 jit_solution(10621958001166463618)
XLA Ops:
  7.2 0.0 all-reduce.4.cloned.1.call-start
  7.2 1.4 fusion.81
  10.5 11.0 broadcast_select_fusion.1
  21.5 0.0 all-reduce.4.cloned.1.call-update
  23.4 11.5 %copy.36 = bf16[2,64,64,512]{3,1,0,2:T(8,128)(2,1)} copy(bf16[2,64,64,512]{3,2,1,0:T(8,128)(2,1)} %param.3) | data formatting | bytes 16777216 | tf_op args[0]
  34.9 0.1 reshape.184
  35.2 5.7 fusion.9
  40.9 0.5 convert_bitcast_fusion.2
  41.4 0.1 fusion.79
  41.6 0.2 slice_bitcast_fusion.8
  41.8 1.2 maximum_bitcast_fusion.10
  42.9 1.5 pad_maximum_fusion.2
  44.5 1.3 slice-done.1
  45.8 2.3 fusion.8
  48.1 0.7 convert_bitcast_fusion.3
  48.8 0.1 fusion.78
  49.0 0.2 slice_bitcast_fusion.10
  49.2 1.2 maximum_bitcast_fusion.8
  50.4 1.5 pad_maximum_fusion.1
  51.9 2.3 fusion.10
  54.2 0.5 convert_bitcast_fusion.1
  54.7 0.1 fusion.80
  54.9 0.2 slice_bitcast_fusion.6
  55.1 1.2 maximum_bitcast_fusion.12
  56.2 1.5 pad_maximum_fusion.3
  57.8 11.7 %copy_convert_fusion = f32[2,64,64,512]{3,2,0,1:T(8,128)} fusion(bf16[2,64,64,512]{3,2,1,0:T(8,128)(2,1)} %param.3), kind=kLoop, calls=%fused_computation.16 | loop fusion | flops 4194304 | bytes 25165824 | tf_op jit(solution)/shard_map/convert_element_type | solution.py:79
  69.5 510.7 %all-reduce.4.cloned.1.call-done = (bf16[2,64,64,512]{3,2,1,0:T(8,128)(2,1)}, bf16[2,64,64,512]{3,2,1,0:T(8,128)(2,1)}, bf16[2,64,64,512]{3,2,1,0:T(8,128)(2,1)}) async-done(((bf16[2,64,64,512]{3,2,1,0:T(8,128)(2,1)}, bf16[2,64,64,512]{3,2,1,0:T(8,128)(2,1)}, bf16[2,64,64,512]{3,2,1,0:T(8,128)(2,1)}), (bf16[2,64,64,512]{3,2,1,0:T(8,128)(2,1)}, bf16[2,64,64,512]{3,2,1,0:T(8,128)(2,1)}, ...) | async-done | bytes 25165840 | tf_op jit(solution)/shard_map/psum | solution.py:18
  580.2 4.0 slice_bitcast_fusion.5
  584.2 11.2 slice_bitcast_fusion.1
  595.4 10.3 fusion.3
  605.7 10.2 fusion
  615.8 20.8 %convert_bitcast_fusion = f32[2,64,64,512]{3,2,0,1:T(8,128)} fusion(bf16[64,64,512]{2,1,0:T(8,128)(2,1)} %get-tuple-element.17, bf16[64,64,512]{2,1,0:T(8,128)(2,1)S(1)} %copy-done, f32[64,512,2,64]{1,3,2,0:T(8,128)} %fusion, f32[64,512,2,64]{1,3,2,0:T(8,128)} %fusion.3, bf16[2,64,64,128]{3,1,2,0:T(8,128)(2,1)} %pad_maximum_fusion.3), kind=kOutput, calls=%fused_computation.1 | convolution fusion | flops 1111490560 | bytes 60817408 | tf_op jit(solution)/shard_map/cfsk,fkr->cfsr/dot_general | solution.py:65
  636.7 13.9 %subtract_reduce_fusion = (f32[64,64]{1,0:T(8,128)S(1)}, f32[64,64]{1,0:T(8,128)S(1)}, f32[64,64]{1,0:T(8,128)S(1)}) fusion(f32[2,64,64,512]{3,2,0,1:T(8,128)} %copy_convert_fusion, f32[2,64,64,512]{3,2,0,1:T(8,128)} %convert_bitcast_fusion), kind=kLoop, calls=%fused_computation.19 | loop fusion | flops 25153536 | bytes 33603584 | tf_op jit(solution)/shard_map/reduce_sum | solution.py:82
  650.6 0.4 fusion.33
  651.0 0.4 fusion.50
  651.4 0.4 convolution_subtract_fusion
  651.8 13.8 %all-reduce = (f32[64,31]{0,1:T(8,128)S(1)}, f32[64,31]{0,1:T(8,128)S(1)}) all-reduce(f32[64,31]{0,1:T(8,128)S(1)} %fusion.33, f32[64,31]{0,1:T(8,128)S(1)} %convolution_subtract_fusion), channel_id=1, replica_groups=mesh['shot'=32,'freq'=4] {'freq'}, use_global_device_ids=true, to_apply=%region_4.5 | all-reduce | flops 3968 | bytes 31744 | tf_op jit(solution)/shard_map/psum | solution.py:92
  665.6 2.9 gather_fusion
  668.6 1.0 copy.45
  669.5 1.0 copy.46
  670.5 1.2 fusion.18
  671.7 182.3 %custom-call.9 = f32[64,31,31]{2,1,0:T(8,128)S(1)} custom-call(f32[64,31,31]{2,1,0:T(8,128)} %fusion.18), custom_call_target="Cholesky" | custom-call | tf_op jit(solution)/shard_map/jit(cholesky)/cholesky | solution.py:32
  854.0 0.6 copy.47
  854.7 0.2 select_reduce_fusion
  854.9 0.2 select_bitcast_fusion
  855.1 11.7 %custom-call.10 = f32[64,1,31,31]{0,2,3,1:T(8,128)S(1)} custom-call(f32[64,1,31,31]{0,3,2,1:T(8,128)S(1)} %select_bitcast_fusion), custom_call_target="InvertDiagBlocksLowerTriangular" | custom-call | tf_op jit(solution)/shard_map/triangular_solve | solution.py:34
  866.8 0.1 broadcast_add_fusion
  866.9 0.1 fusion.25
  867.0 0.1 fusion.26
  867.1 0.3 fusion.48
  867.4 0.4 convolution_negate_fusion
  867.8 13.7 %subtract_convert_fusion.1 = (bf16[1,64,64,512]{3,2,0,1:T(8,128)(2,1)S(1)}, bf16[1,64,64,512]{3,2,0,1:T(8,128)(2,1)}) fusion(f32[2,64,64,512]{3,2,0,1:T(8,128)} %copy_convert_fusion, f32[2,64,64,512]{3,2,0,1:T(8,128)} %convert_bitcast_fusion, f32[64,64]{1,0:T(8,128)S(1)} %convolution_negate_fusion, f32[64,64]{1,0:T(8,128)S(1)} %fusion.48), kind=kLoop, calls=%fused_computation.18 | loop fusion | flops 20971520 | bytes 41975808 | tf_op jit(solution)/shard_map/convert.2
  881.5 6.4 pad_maximum_fusion
  887.9 34.3 %copy.49 = bf16[2,64,64,512]{2,0,1,3:T(2,128)(2,1)} copy(bf16[2,64,64,512]{3,2,0,1:T(8,128)(2,1)} %pad_maximum_fusion) | data formatting | bytes 16777216 | tf_op jit(solution)/shard_map/stack | solution.py:98
  922.2 16.6 %reshape.205 = bf16[4,2,524288]{2,1,0:T(2,128)(2,1)} reshape(bf16[512,64,2,64]{3,2,1,0:T(2,128)(2,1)} %bitcast.133) | data formatting | bytes 16777216
  938.8 8.4 all-to-all-start
  947.1 2.2 multiply_convert_fusion.1
  949.3 0.1 pad_maximum_fusion.4
  949.4 91.6 %all-to-all-done = bf16[4,2,524288]{2,1,0:T(2,128)(2,1)} async-done(((bf16[4,2,524288]{2,1,0:T(2,128)(2,1)}), bf16[4,2,524288]{2,1,0:T(2,128)(2,1)}, u32[]{:S(2)}, u32[]{:S(2)}) %all-to-all-start) | async-done | bytes 8388640 | tf_op jit(solution)/shard_map/all_to_all | solution.py:100
  1041.0 16.0 %reshape.206 = bf16[512,64,2,64]{3,2,1,0:T(2,128)(2,1)} reshape(bf16[4,2,524288]{2,1,0:T(2,128)(2,1)} %all-to-all-done) | data formatting | bytes 16777216
  1056.9 34.3 %copy.50 = bf16[2,64,64,4,128]{4,2,1,3,0:T(8,128)(2,1)} copy(bf16[2,64,64,4,128]{2,0,1,4,3:T(2,128)(2,1)} %bitcast.134) | data formatting | bytes 16777216 | tf_op jit(solution)/shard_map/all_to_all | solution.py:100
  1091.2 23.6 %copy.80 = bf16[64,8,64,128]{3,1,2,0:T(8,128)(2,1)} copy(bf16[64,8,64,128]{3,2,1,0:T(8,128)(2,1)} %bitcast.135) | data formatting | bytes 16777216
  1114.9 12.0 %copy.51 = bf16[8192,512]{1,0:T(8,128)(2,1)} copy(bf16[8192,512]{0,1:T(8,128)(2,1)} %bitcast.136) | data formatting | bytes 16777216 | tf_op jit(solution)/shard_map/dot_general | solution.py:104
  1126.9 10.1 convolution_convert_fusion
  (21 shorter events, 0.2 us)
Async XLA Ops:
  7.2 573.1 %all-reduce.4.cloned.1.call-start = ((), (), s32[]{:S(2)}) async-start(), calls=%async_computation.1 | async-start | bytes 50331648 | tf_op jit(solution)/shard_map/psum | solution.py:18
  23.4 11.7 %copy-start.1 = (s32[64,512]{1,0:T(8,128)S(1)}, s32[64,512]{1,0:T(8,128)}, u32[]{:S(2)}) copy-start(s32[64,512]{1,0:T(8,128)} %param.4) | copy-start | bytes 393220
  41.4 3.1 slice-start
  41.8 4.0 slice-start.1
  605.7 10.2 copy-start
  867.1 14.4 %copy-start.2 = (f32[64,31]{0,1:T(8,128)}, f32[64,31]{0,1:T(8,128)S(1)}, u32[]{:S(2)}) copy-start(f32[64,31]{0,1:T(8,128)S(1)} %fusion.26) | copy-start | bytes 23812
  938.8 102.2 %all-to-all-start = ((bf16[4,2,524288]{2,1,0:T(2,128)(2,1)}), bf16[4,2,524288]{2,1,0:T(2,128)(2,1)}, u32[]{:S(2)}, u32[]{:S(2)}) async-start(bf16[4,2,524288]{2,1,0:T(2,128)(2,1)} %reshape.205), calls=%async_computation | async-start | bytes 16777216 | tf_op jit(solution)/shard_map/all_to_all | solution.py:100
Sparse Core Ops, SparseCore 0:
  21.6 558.5 all-reduce.3
where the time goes:
time: 1160 us; the launch traced here: 1140 us
  waiting for transfers between devices  602 us (52%)
  other arithmetic  265 us (23%)
  local copies, waits for them, and re-layouts  172 us (15%)
  matrix products  63.8 us (6%)
  between operations  18.6 us (2%)
  blocking collectives  13.8 us (1%)
    psum x1, waiting for transfers between devices, broadcast(): return lax.psum(kept, axis)  511 us
    another operation x4, other arithmetic, solve_filters(): factor = jnp.linalg.cholesky(normal)  182 us
    all_to_all x1, waiting for transfers between devices, per_device(): lax.all_to_all(residual, 'freq', split_axis=3, concat_axis=1, tiled=True)  91.6 us
    unnamed x14, local copies, waits for them, and re-layouts  69.1 us
    dot_general x3, matrix products, product_step(): jnp.einsum('cfsk,fkr->cfsr', stacked, right_side, preferred_element_type=...  41.3 us
    another operation x1, local copies, waits for them, and re-layouts, per_device(): residual = jnp.stack([res_real, res_imag]).astype(jnp.bfloat16)  34.3 us
    all_to_all x1, local copies, waits for them, and re-layouts, per_device(): lax.all_to_all(residual, 'freq', split_axis=3, concat_axis=1, tiled=True)  34.3 us
  transfers between devices with their start and end apart: 2, of which 2 were waited for; matrix products, arithmetic and copies ran while one was open for 4% of the time, Pallas kernels for 0%

commit v1 on v0

v1 whole, which is shorter than its diff:
```python
import math

import jax
import jax.numpy as jnp
import numpy as np
from jax import lax
from jax.experimental import pallas as pl
from jax.experimental.pallas import tpu as pltpu
from jax.sharding import PartitionSpec as P

F = 256
TAPS = 31
STEPS = 3
HALF = (TAPS - 1) // 2
REG = 2.0
N_SHOT = 32
N_FREQ = 4
N_DEV = N_SHOT * N_FREQ
FL = F // N_DEV
SD = 64
R = 512
BLK = 16
MIB = 1 << 20
LIMIT = 60 * MIB
WINDOW = 8
HIGH = lax.Precision.HIGHEST
MESH = pl.DeviceIdType.MESH


def device_freqs():
    dev = np.arange(N_DEV)
    return (dev % N_FREQ)[:, None] * (F // N_FREQ) + (dev // N_FREQ)[:, None] * FL + np.arange(FL)[None, :]


def angle(freq, step):
    return ((freq * step) % (2 * F)).astype(np.float64) * (2.0 * math.pi / (2 * F))


def corr_table():
    freqs = device_freqs().reshape(N_SHOT, N_FREQ, FL)
    lags = np.abs(np.arange(64) - (TAPS - 1))
    taps = np.arange(32) - HALF
    table = np.zeros((N_FREQ, 96, N_SHOT, 8))
    for j in range(FL):
        col = freqs[:, :, j].T[:, None, :]
        table[:, :64, :, 3 * j] = np.cos(angle(col, lags[None, :, None]))
        table[:, 64:, :, 3 * j + 1] = np.cos(angle(col, taps[None, :, None]))
        table[:, 64:, :, 3 * j + 2] = -np.sin(angle(col, taps[None, :, None]))
    return table.reshape(N_FREQ, 96, N_SHOT * 8).astype(np.float32)


def resp_table():
    freqs = device_freqs().reshape(N_SHOT, N_FREQ, FL)
    taps = np.arange(32) - HALF
    valid = np.arange(32) < TAPS
    table = np.zeros((N_FREQ, N_SHOT, 8, 32))
    for j in range(FL):
        ang = angle(freqs[:, :, j].T[:, :, None], taps[None, None, :])
        table[:, :, j] = np.cos(ang) * valid
        table[:, :, FL + j] = -np.sin(ang) * valid
    return table.reshape(N_FREQ, N_SHOT * 8, 32).astype(np.float32)


def time_table():
    freqs = device_freqs()
    ang = angle(freqs[:, :, None], np.arange(2 * F)[None, None, :])
    norm = 1.0 / math.sqrt(F)
    table = np.stack([np.cos(ang) * norm, -np.sin(ang) * norm], axis=1)
    return table.reshape(2 * F, 2 * F).astype(np.float32)


def predict_kernel(gain, owners_ref, c_ref, x_ref, oa_ref, ob_ref, oc_ref, pred_ref, corr_ref, w_ref):
    @pl.when(pl.program_id(0) == 0)
    def _():
        for j in range(FL):
            for t, o_ref in enumerate((oa_ref, ob_ref, oc_ref)):
                real, imag = o_ref[0, 0, j], o_ref[0, 1, j]
                top = slice(t * SD, (t + 1) * SD)
                under = 3 if t == 2 else 4 + t
                low = slice(under * SD, (under + 1) * SD)
                w_ref[j, top, :R] = real
                w_ref[j, top, R:] = imag
                w_ref[j, low, :R] = -imag
                w_ref[j, low, R:] = real

    n = c_ref.shape[0]
    rows = n * SD
    lane = lax.broadcasted_iota(jnp.int32, (rows, 128), 1)
    cols = jnp.zeros((rows, 128), jnp.float32)
    for j in range(FL):
        lhs = c_ref[:, j].reshape(rows, 2 * STEPS * SD)
        acc = jnp.dot(lhs, w_ref[j], preferred_element_type=jnp.float32)
        pred = (gain * acc).astype(jnp.bfloat16)
        pr, pi = pred[:, :R], pred[:, R:]
        pred_ref[:, 0, j] = pr.reshape(n, SD, R)
        pred_ref[:, 1, j] = pi.reshape(n, SD, R)
        pr, pi = pr.astype(jnp.float32), pi.astype(jnp.float32)
        xr = x_ref[:, 0, j].reshape(rows, R).astype(jnp.float32)
        xi = x_ref[:, 1, j].reshape(rows, R).astype(jnp.float32)
        spec = jnp.sum(pr * pr + pi * pi, axis=1, keepdims=True)
        cr = jnp.sum(pr * xr + pi * xi, axis=1, keepdims=True)
        ci = jnp.sum(pr * xi - pi * xr, axis=1, keepdims=True)
        for q, col in enumerate((spec, cr, ci)):
            cols = jnp.where(lane == 3 * j + q, col, cols)
    flat = cols.T[:8]
    for m in range(n):
        pair = flat[:, (m // 2) * 128 : (m // 2) * 128 + 128]
        corr_ref[m] = pair if m % 2 == 0 else pltpu.roll(pair, SD, 1)


def predict(owners, coeffs, data, gain):
    step = 4
    grid = N_SHOT // step
    owner_spec = [
        pl.BlockSpec((1, 2, FL, SD, R), lambda i, ow, t=t: (ow[t], 0, 0, 0, 0)) for t in range(STEPS)
    ]
    return pl.pallas_call(
        lambda *refs: predict_kernel(gain, *refs),
        grid_spec=pltpu.PrefetchScalarGridSpec(
            num_scalar_prefetch=1,
            grid=(grid,),
            in_specs=[
                pl.BlockSpec((step, FL, SD, 2 * STEPS * SD), lambda i, ow: (i, 0, 0, 0)),
                pl.BlockSpec((step, 2, FL, SD, R), lambda i, ow: (i, 0, 0, 0, 0)),
            ]
            + owner_spec,
            out_specs=[
                pl.BlockSpec((step, 2, FL, SD, R), lambda i, ow: (i, 0, 0, 0, 0)),
                pl.BlockSpec((step, 8, 128), lambda i, ow: (i, 0, 0)),
            ],
            scratch_shapes=[pltpu.VMEM((FL, 2 * STEPS * SD, 2 * R), jnp.bfloat16)],
        ),
        out_shape=(
            jax.ShapeDtypeStruct(data.shape, jnp.bfloat16),
            jax.ShapeDtypeStruct((N_SHOT, 8, 128), jnp.float32),
        ),
        compiler_params=pltpu.CompilerParams(
            dimension_semantics=("arbitrary",), vmem_limit_bytes=LIMIT
        ),
        cost_estimate=pl.CostEstimate(flops=4 * 10**9, bytes_accessed=28 * 10**6, transcendentals=0),
        name="predict",
    )(owners, coeffs, data, data, data, data)


def signed(flip, offset, size):
    return jnp.where(flip == 1, lax.rem(size - offset, size), offset)


def shot_peer_of(me, me_freq, n):
    x, z, y = me // 16, lax.rem(me // 4, 4), lax.rem(me, 4)
    flip = lax.rem(lax.rem(me_freq, 2) + x + y + z, 2)
    d = lax.rem(n * 11, N_SHOT)
    x = lax.rem(x + d // 16, 2)
    z = lax.rem(z + signed(flip, lax.rem(d // 4, 4), 4), 4)
    y = lax.rem(y + signed(flip, lax.rem(d, 4), 4), 4)
    return x * 16 + z * 4 + y


def any_peer_of(me, me_freq, n):
    core = lax.rem(me_freq, 2)
    d = lax.rem(n * 43, N_DEV)
    x = lax.rem((me_freq // 2) * 2 + me // 16 + signed(core, lax.rem(d // 16, 4), 4), 4)
    z = lax.rem(lax.rem(me // 4, 4) + signed(core, lax.rem(d // 4, 4), 4), 4)
    y = lax.rem(lax.rem(me, 4) + signed(core, lax.rem(d, 4), 4), 4)
    other = lax.rem(core + d // 64, 2)
    return lax.rem(x, 2) * 16 + z * 4 + y, (x // 2) * 2 + other


def greet(me, me_freq, with_freq, with_all):
    barrier = pltpu.get_barrier_semaphore()

    def shot_peer(n, carry):
        peer = shot_peer_of(me, me_freq, n)
        pl.semaphore_signal(barrier, 1, device_id=(peer, me_freq), device_id_type=MESH)
        return carry

    def any_peer(n, carry):
        pl.semaphore_signal(barrier, 1, device_id=any_peer_of(me, me_freq, n), device_id_type=MESH)
        return carry

    if with_all:
        lax.fori_loop(1, N_DEV, any_peer, 0)
        pl.semaphore_wait(barrier, N_DEV - 1)
        return
    lax.fori_loop(1, N_SHOT, shot_peer, 0)
    count = N_SHOT - 1
    if with_freq:
        for e in range(1, N_FREQ):
            pl.semaphore_signal(
                barrier, 1, device_id=(me, lax.rem(me_freq + e, N_FREQ)), device_id_type=MESH
            )
        count += N_FREQ - 1
    pl.semaphore_wait(barrier, count)


def exchange_kernel(
    owners_ref, rec_ref, shot_ref, x_ref, c_ref,
    block, wide, narrow, coeffs, load_sem, own_sem, send_sem, recv_sem, csend_sem, crecv_sem,
):
    me = lax.axis_index("shot")
    me_freq = lax.axis_index("freq")
    freqs = rec_ref.shape[1]
    rows = 2 * freqs

    def load(b):
        return pltpu.make_async_copy(
            rec_ref.at[:, :, pl.ds(b * BLK, BLK), :], block.at[b % 2], load_sem.at[b % 2]
        )

    def data_copy(d):
        peer = shot_peer_of(me, me_freq, d)
        return pltpu.make_async_remote_copy(
            src_ref=rec_ref.at[:, pl.ds(peer * FL, FL)],
            dst_ref=x_ref.at[me],
            send_sem=send_sem.at[d],
            recv_sem=recv_sem.at[d],
            device_id=(peer, me_freq),
            device_id_type=MESH,
        )

    def coeff_copy(d):
        peer = shot_peer_of(me, me_freq, d)
        return pltpu.make_async_remote_copy(
            src_ref=coeffs.at[pl.ds(peer * FL, FL)],
            dst_ref=c_ref.at[me],
            send_sem=csend_sem.at[d],
            recv_sem=crecv_sem.at[d],
            device_id=(peer, me_freq),
            device_id_type=MESH,
        )

    def run(action):
        def body(d, carry):
            action(d)
            return carry

        lax.fori_loop(1, N_SHOT, body, 0)

    def send_next(copy, d):
        copy(d - WINDOW).wait_send()
        copy(d).start()

    load(0).start()
    greet(me, me_freq, False, False)
    for d in range(1, WINDOW + 1):
        data_copy(d).start()
    own = pltpu.make_async_copy(rec_ref.at[:, pl.ds(me * FL, FL)], x_ref.at[me], own_sem.at[0])
    own.start()

    slot = lax.broadcasted_iota(jnp.int32, (4 * SD, R), 0)
    key = jnp.where(slot < SD, owners_ref[0] * SD + slot, owners_ref[1] * SD + slot - SD)
    key = jnp.where(slot < 2 * SD, key, owners_ref[2] * SD + slot - 2 * SD)
    key = jnp.where(slot < 3 * SD, key, -1)
    for b in range(SD // BLK):
        if b + 1 < SD // BLK:
            load(b + 1).start()
        load(b).wait()
        for ch in range(R // 128):
            part = block[b % 2, :, :, :, ch * 128 : (ch + 1) * 128]
            wide[ch] = part.astype(jnp.float32).reshape(rows * BLK, 128)

        def bin_shot(m, carry):
            data = jnp.concatenate(
                [wide[ch, pl.ds(m, rows, stride=BLK), :] for ch in range(R // 128)], axis=1
            ).astype(jnp.bfloat16)
            where = shot_ref[pl.ds(b * BLK + m, 1), :]
            one_hot = (jnp.broadcast_to(where, key.shape) == key).astype(jnp.bfloat16)
            out = lax.dot_general(
                data, one_hot, (((1,), (1,)), ((), ())), preferred_element_type=jnp.float32
            )
            real, imag = out[:freqs], out[freqs:]
            narrow[0, pl.ds(m, freqs, stride=BLK), :] = real[:, :128]
            narrow[1, pl.ds(m, freqs, stride=BLK), :] = real[:, 128:] + pltpu.roll(imag[:, 128:], SD, 1)
            narrow[2, pl.ds(m, freqs, stride=BLK), :] = imag[:, :128]
            due = b * BLK + m

            @pl.when((lax.rem(due, 2) == 0) & (due // 2 + WINDOW + 1 < N_SHOT))
            def _():
                send_next(data_copy, due // 2 + WINDOW + 1)

            return carry

        lax.fori_loop(0, BLK, bin_shot, 0)
        for ch in range(3):
            part = narrow[ch].reshape(freqs, BLK, 128).astype(jnp.bfloat16)
            coeffs[:, b * BLK : (b + 1) * BLK, ch * 128 : (ch + 1) * 128] = part
    mine = pltpu.make_async_copy(coeffs.at[pl.ds(me * FL, FL)], c_ref.at[me], own_sem.at[1])
    mine.start()

    def data_to_coeff(d, carry):
        data_copy(N_SHOT - 1 - WINDOW + d).wait_send()
        coeff_copy(d).start()
        return carry

    def coeff_step(d, carry):
        send_next(coeff_copy, d)
        return carry

    def coeff_end(d, carry):
        coeff_copy(d).wait_send()
        return carry

    lax.fori_loop(1, WINDOW + 1, data_to_coeff, 0)
    lax.fori_loop(WINDOW + 1, N_SHOT, coeff_step, 0)
    lax.fori_loop(N_SHOT - WINDOW, N_SHOT, coeff_end, 0)
    own.wait()
    mine.wait()
    run(lambda d: data_copy(d).wait_recv())
    run(lambda d: coeff_copy(d).wait_recv())


def exchange(owners, recorded, rec_shot):
    freqs = recorded.shape[1]
    width = 2 * STEPS * SD
    anywhere = pl.BlockSpec(memory_space=pl.ANY)
    return pl.pallas_call(
        exchange_kernel,
        in_specs=[
            pl.BlockSpec(memory_space=pltpu.SMEM),
            anywhere,
            pl.BlockSpec(memory_space=pltpu.VMEM),
        ],
        out_specs=[anywhere, anywhere],
        out_shape=(
            jax.ShapeDtypeStruct((N_SHOT, 2, FL, SD, R), jnp.bfloat16),
            jax.ShapeDtypeStruct((N_SHOT, FL, SD, width), jnp.bfloat16),
        ),
        scratch_shapes=[
            pltpu.VMEM((2, 2, freqs, BLK, R), jnp.bfloat16),
            pltpu.VMEM((R // 128, 2 * freqs * BLK, 128), jnp.float32),
            pltpu.VMEM((3, freqs * BLK, 128), jnp.float32),
            pltpu.VMEM((freqs, SD, width), jnp.bfloat16),
            pltpu.SemaphoreType.DMA((2,)),
            pltpu.SemaphoreType.DMA((2,)),
            pltpu.SemaphoreType.DMA((N_SHOT,)),
            pltpu.SemaphoreType.DMA((N_SHOT,)),
            pltpu.SemaphoreType.DMA((N_SHOT,)),
            pltpu.SemaphoreType.DMA((N_SHOT,)),
        ],
        compiler_params=pltpu.CompilerParams(
            collective_id=0, has_side_effects=True, vmem_limit_bytes=LIMIT
        ),
        name="exchange",
    )(owners, recorded, rec_shot)


def filter_kernel(
    damping, corr_ref, ct_ref, rt_ref, filt_ref, resp_ref,
    arrived, parts, answer, ext_ref, send_sem, recv_sem, fsend_sem, frecv_sem, rsend_sem, rrecv_sem,
):
    me = lax.axis_index("shot")
    me_freq = lax.axis_index("freq")

    def corr_copy(d):
        peer = shot_peer_of(me, me_freq, d)
        return pltpu.make_async_remote_copy(
            src_ref=corr_ref.at[peer],
            dst_ref=arrived.at[me],
            send_sem=send_sem.at[d],
            recv_sem=recv_sem.at[d],
            device_id=(peer, me_freq),
            device_id_type=MESH,
        )

    def part_copy(e):
        return pltpu.make_async_remote_copy(
            src_ref=parts.at[me_freq],
            dst_ref=parts.at[me_freq],
            send_sem=fsend_sem.at[e],
            recv_sem=frecv_sem.at[e],
            device_id=(me, lax.rem(me_freq + e, N_FREQ)),
            device_id_type=MESH,
        )

    def resp_copy(d):
        peer = shot_peer_of(me, me_freq, d)
        return pltpu.make_async_remote_copy(
            src_ref=answer.at[peer],
            dst_ref=resp_ref.at[me],
            send_sem=rsend_sem.at[d],
            recv_sem=rrecv_sem.at[d],
            device_id=(peer, me_freq),
            device_id_type=MESH,
        )

    def run(action):
        def body(d, carry):
            action(d)
            return carry

        lax.fori_loop(1, N_SHOT, body, 0)

    greet(me, me_freq, True, False)
    run(lambda d: corr_copy(d).start())
    arrived[me] = corr_ref[me]
    run(lambda d: corr_copy(d).wait())
    parts[me_freq] = jnp.dot(
        ct_ref[...],
        arrived[...].reshape(N_SHOT * 8, 128),
        precision=HIGH,
        preferred_element_type=jnp.float32,
    )
    for e in range(1, N_FREQ):
        part_copy(e).start()
    for e in range(1, N_FREQ):
        part_copy(e).wait()
    total = parts[0]
    for e in range(1, N_FREQ):
        total = total + parts[e]

    row64 = lax.broadcasted_iota(jnp.int32, (64, 128), 0)
    row = lax.broadcasted_iota(jnp.int32, (32, 128), 0)
    ext_ref[...] = total[:64] + jnp.where(row64 == TAPS - 1, damping, 0.0)
    rhs = total[64:] + jnp.where(row == HALF, damping, 0.0)
    cols = [ext_ref[pl.ds(TAPS - 1 - k, 32), :] for k in range(TAPS)]
    inverse = []
    for p in range(TAPS):
        inv = 1.0 / cols[p][p : p + 1, :]
        inverse.append(inv)
        if p == TAPS - 1:
            break
        factor = jnp.where(row > p, cols[p] * inv, 0.0)
        rhs = rhs - factor * rhs[p : p + 1, :]
        for k in range(p + 1, TAPS):
            cols[k] = cols[k] - factor * cols[k][p : p + 1, :]
    found = jnp.zeros((32, 128), jnp.float32)
    for p in range(TAPS - 1, -1, -1):
        value = rhs[p : p + 1, :] * inverse[p]
        found = jnp.where(row == p, value, found)
        rhs = rhs - cols[p] * value
    resp = jnp.dot(rt_ref[...], found, precision=HIGH, preferred_element_type=jnp.float32)
    answer[...] = resp.reshape(N_SHOT, 8, 128)
    run(lambda d: resp_copy(d).start())
    resp_ref[me] = answer[me]
    filt_ref[...] = jnp.concatenate([found, jnp.zeros((96, 128), jnp.float32)], axis=0).T[:SD]
    run(lambda d: resp_copy(d).wait())


def match(corr, ct, rt, damping):
    return pl.pallas_call(
        lambda *refs: filter_kernel(damping, *refs),
        in_specs=[pl.BlockSpec(memory_space=pltpu.VMEM)] * 3,
        out_specs=[pl.BlockSpec(memory_space=pltpu.VMEM)] * 2,
        out_shape=(
            jax.ShapeDtypeStruct((SD, 128), jnp.float32),
            jax.ShapeDtypeStruct((N_SHOT, 8, 128), jnp.float32),
        ),
        scratch_shapes=[
            pltpu.VMEM((N_SHOT, 8, 128), jnp.float32),
            pltpu.VMEM((N_FREQ, 96, 128), jnp.float32),
            pltpu.VMEM((N_SHOT, 8, 128), jnp.float32),
            pltpu.VMEM((64, 128), jnp.float32),
            pltpu.SemaphoreType.DMA((N_SHOT,)),
            pltpu.SemaphoreType.DMA((N_SHOT,)),
            pltpu.SemaphoreType.DMA((N_FREQ,)),
            pltpu.SemaphoreType.DMA((N_FREQ,)),
            pltpu.SemaphoreType.DMA((N_SHOT,)),
            pltpu.SemaphoreType.DMA((N_SHOT,)),
        ],
        compiler_params=pltpu.CompilerParams(
            collective_id=1, has_side_effects=True, vmem_limit_bytes=16 * MIB
        ),
        name="match",
    )(corr, ct, rt)


def residual_kernel(
    x_ref, p_ref, resp_ref, out_ref, xb, pb, sb, load_sem, own_sem, send_sem, recv_sem
):
    me = lax.axis_index("shot")
    me_freq = lax.axis_index("freq")
    mine = me * N_FREQ + me_freq
    width = R // N_FREQ
    diagonal = lax.broadcasted_iota(jnp.int32, (SD, 128), 0) == lax.broadcasted_iota(
        jnp.int32, (SD, 128), 1
    )
    load_x = pltpu.make_async_copy(x_ref, xb, load_sem.at[0])
    load_p = pltpu.make_async_copy(p_ref, pb, load_sem.at[1])

    def copy(n):
        return pltpu.make_async_remote_copy(
            src_ref=sb.at[n],
            dst_ref=out_ref.at[mine],
            send_sem=send_sem.at[n],
            recv_sem=recv_sem.at[n],
            device_id=any_peer_of(me, me_freq, n),
            device_id_type=MESH,
        )

    def compute(n):
        shot, freq = any_peer_of(me, me_freq, n)
        resp = resp_ref[shot]
        part = pl.ds(pl.multiple_of(freq * width, width), width)

        def column(q):
            spread = jnp.broadcast_to(resp[q : q + 1], (SD, 128))
            return jnp.sum(jnp.where(diagonal, spread, 0.0), axis=1, keepdims=True)

        for j in range(FL):
            real, imag = column(j), column(FL + j)
            xr = xb[shot, 0, j, :, part].astype(jnp.float32)
            xi = xb[shot, 1, j, :, part].astype(jnp.float32)
            pr = pb[shot, 0, j, :, part].astype(jnp.float32)
            pi = pb[shot, 1, j, :, part].astype(jnp.float32)
            sb[n, 0, j] = (xr - (real * pr - imag * pi)).astype(jnp.bfloat16)
            sb[n, 1, j] = (xi - (real * pi + imag * pr)).astype(jnp.bfloat16)

    load_x.start()
    load_p.start()
    greet(me, me_freq, False, True)
    load_x.wait()
    load_p.wait()

    def step(n, carry):
        compute(n)
        copy(n).start()
        return carry

    lax.fori_loop(1, N_DEV, step, 0)
    compute(0)
    own = pltpu.make_async_copy(sb.at[0], out_ref.at[mine], own_sem.at[0])
    own.start()
    own.wait()

    def finish(n, carry):
        copy(n).wait()
        return carry

    lax.fori_loop(1, N_DEV, finish, 0)


def residual(data, pred, resp):
    width = R // N_FREQ
    anywhere = pl.BlockSpec(memory_space=pl.ANY)
    return pl.pallas_call(
        residual_kernel,
        in_specs=[anywhere, anywhere, pl.BlockSpec(memory_space=pltpu.VMEM)],
        out_specs=anywhere,
        out_shape=jax.ShapeDtypeStruct((N_DEV, 2, FL, SD, width), jnp.bfloat16),
        scratch_shapes=[
            pltpu.VMEM((N_SHOT, 2, FL, SD, R), jnp.bfloat16),
            pltpu.VMEM((N_SHOT, 2, FL, SD, R), jnp.bfloat16),
            pltpu.VMEM((N_DEV, 2, FL, SD, width), jnp.bfloat16),
            pltpu.SemaphoreType.DMA((2,)),
            pltpu.SemaphoreType.DMA((1,)),
            pltpu.SemaphoreType.DMA((N_DEV,)),
            pltpu.SemaphoreType.DMA((N_DEV,)),
        ],
        compiler_params=pltpu.CompilerParams(
            collective_id=2, has_side_effects=True, vmem_limit_bytes=LIMIT
        ),
        name="residual",
    )(data, pred, resp)


def transform_kernel(r_ref, t_ref, *rest):
    out_ref, wide_ref = rest[-2:]
    k = r_ref.shape[0]
    s = r_ref.shape[1]
    wide_ref[...] = r_ref[...].astype(jnp.float32).reshape(k * s, 128)
    group = 4
    for m in range(0, s, group):
        rows = jnp.concatenate(
            [wide_ref[pl.ds(m + g, k, stride=s), :].T.astype(jnp.bfloat16) for g in range(group)], axis=0
        )
        out = jnp.dot(rows, t_ref[...], preferred_element_type=jnp.float32).astype(jnp.bfloat16)
        out_ref[m : m + group] = out.reshape(group, 128, 2 * F)


def transform(spectra, table, chunk, before):
    k, shots, recv = spectra.shape
    step = 16
    base = chunk * (shots // step)
    in_specs = [
        pl.BlockSpec((k, step, recv), lambda i: (0, i, 0)),
        pl.BlockSpec((k, 2 * F), lambda i: (0, 0)),
    ]
    args = [spectra, table]
    alias = {}
    if before is not None:
        in_specs.append(pl.BlockSpec(memory_space=pl.ANY))
        args.append(before)
        alias = {2: 0}
    return pl.pallas_call(
        transform_kernel,
        grid=(shots // step,),
        in_specs=in_specs,
        out_specs=pl.BlockSpec((step, recv, 2 * F), lambda i: (i + base, 0, 0)),
        out_shape=jax.ShapeDtypeStruct((SD, recv, 2 * F), jnp.bfloat16),
        scratch_shapes=[pltpu.VMEM((k * step, recv), jnp.float32)],
        input_output_aliases=alias,
        compiler_params=pltpu.CompilerParams(
            dimension_semantics=("arbitrary",), vmem_limit_bytes=LIMIT
        ),
        cost_estimate=pl.CostEstimate(flops=2 * 10**9, bytes_accessed=12 * 10**6, transcendentals=0),
        name=f"transform{chunk}",
    )(*args)


def per_device(recorded, rec_shot, owners):
    gain = (N_SHOT / (2.0 * R * STEPS)) ** 0.5
    me_freq = lax.axis_index("freq")
    ct = lax.dynamic_index_in_dim(jnp.asarray(corr_table()), me_freq, 0, False)
    rt = lax.dynamic_index_in_dim(jnp.asarray(resp_table()), me_freq, 0, False)
    data, coeffs = exchange(owners, recorded, rec_shot)
    pred, corr = predict(owners, coeffs, data, gain)
    filt, resp = match(corr, ct, rt, REG * R * F)
    res = residual(data, pred, resp)
    table = jnp.asarray(time_table(), dtype=jnp.bfloat16)
    primaries = transform(res.reshape(2 * F, SD, R // N_FREQ), table, 0, None)
    return (primaries, filt[:, :TAPS])


def solution(mesh):
    placed = (P(None, "freq", "shot", None), P("shot", None), P())
    return jax.shard_map(
        per_device,
        mesh=mesh,
        in_specs=placed,
        out_specs=(P("shot", "freq", None), P("shot", None)),
        check_vma=False,
    )
```

time: 1160 us -> 343 us (0.30); the launches traced: 1140 us -> 341 us
  waiting for transfers between devices: 602 us -> 0 us
  Pallas kernels: 0 us -> 336 us
  other arithmetic: 265 us -> 0 us
  local copies, waits for them, and re-layouts: 172 us -> 4.05 us
  matrix products: 63.8 us -> 0 us
  between operations: 18.6 us -> 0.67 us
  blocking collectives: 13.8 us -> 0 us
    psum x1 -> x0, waiting for transfers between devices: 511 us -> none  [broadcast(): return lax.psum(kept, axis)]
    pallas_call x0 -> x5, Pallas kernels: none -> 336 us  [the longest x1 165 us: exchange(): pl.pallas_call(exchange_kernel, in_specs=[pl.BlockSpec(memory_space=pltpu...]
    another operation x18 -> x0, other arithmetic: 225 us -> none  [the longest x4 182 us: solve_filters(): factor = jnp.linalg.cholesky(normal)]
    all_to_all x1 -> x0, waiting for transfers between devices: 91.6 us -> none  [per_device(): lax.all_to_all(residual, 'freq', split_axis=3, concat_axis=1, tiled=True)]
    unnamed x14 -> x5, local copies, waits for them, and re-layouts: 69.1 us -> 2.23 us
    dot_general x9 -> x0, matrix products: 53.3 us -> none  [the longest x3 41.3 us: product_step(): jnp.einsum('cfsk,fkr->cfsr', stacked, right_side, preferred_element_type=...]
    another operation x2 -> x0, local copies, waits for them, and re-layouts: 35 us -> none  [the longest x1 34.3 us: per_device(): residual = jnp.stack([res_real, res_imag]).astype(jnp.bfloat16)]
    all_to_all x1 -> x0, local copies, waits for them, and re-layouts: 34.3 us -> none  [per_device(): lax.all_to_all(residual, 'freq', split_axis=3, concat_axis=1, tiled=True)]
  transfers between devices with their start and end apart: 2 -> 0, of which waited for: 2 -> 0; matrix products, arithmetic and copies ran while one was open for 4% -> 0% of each run, Pallas kernels for 0% -> 0%
where the time goes in v1:
time: 343 us; the launch traced here: 341 us
  Pallas kernels  336 us (98%)
  local copies, waits for them, and re-layouts  4.05 us (1%)
    pallas_call x1, Pallas kernels, exchange(): pl.pallas_call(exchange_kernel, in_specs=[pl.BlockSpec(memory_space=pltpu...  165 us
    pallas_call x1, Pallas kernels, residual(): pl.pallas_call(residual_kernel, in_specs=[anywhere, anywhere, pl.BlockSpe...  111 us
    pallas_call x1, Pallas kernels, match(): pl.pallas_call(lambda *refs: filter_kernel(damping, *refs), in_specs=[pl....  33.5 us
    pallas_call x1, Pallas kernels, predict(): pl.pallas_call(lambda *refs: predict_kernel(gain, *refs), grid_spec=pltpu...  14.4 us
    pallas_call x1, Pallas kernels, transform(): pl.pallas_call(transform_kernel, grid=(shots // step,), in_specs=in_specs...  13.1 us

profile of v1, /device:TPU:1, one launch (start us, length us, event | category | flops | bytes accessed | tf_op | source)
XLA Modules:
  0.0 341.1 jit_solution(396252305013370698)
XLA Ops:
  0.6 0.9 dynamic-slice_bitcast_fusion.1.refs_1_
  1.5 0.9 dynamic-slice_bitcast_fusion.refs_2_
  2.5 164.6 %exchange.1 = (bf16[32,2,2,64,512]{4,3,2,1,0:T(8,128)(2,1)}, bf16[32,2,64,384]{3,2,1,0:T(8,128)(2,1)}) custom-call(s32[3]{0:T(128)} %refs_0_.1, bf16[2,64,64,512]{3,2,1,0:T(8,128)(2,1)} %rec_ref.1, s32[64,512]{1,0:T(8,128)} %shot_ref.1), custom_call_target="tpu_custom_call" | custom-call | tf_op jit(solution)/shard_map/exchange/pallas_call | solution.py:316
  167.0 14.4 %predict.1 = (bf16[32,2,2,64,512]{4,3,2,1,0:T(8,128)(2,1)}, f32[32,8,128]{2,1,0:T(8,128)}) custom-call(s32[3]{0:T(128)} %refs_0_.1, bf16[32,2,64,384]{3,2,1,0:T(8,128)(2,1)} %get-tuple-element.9.refs_1_, bf16[32,2,2,64,512]{4,3,2,1,0:T(8,128)(2,1)} %get-tuple-element.8.refs_2_.refs_3_.refs_4_.refs_5_.x_ref, ...), custom_call_target="tpu_custom_call" | custom-call | flops 4000000000 | bytes 28000000 | tf_op jit(solution)/shard_map/predict/pallas_call | solution.py:117
  181.5 0.0 copy-start.1
  181.5 0.9 copy-done.1
  182.4 33.5 %match.1 = (f32[64,128]{1,0:T(8,128)S(1)}, f32[32,8,128]{2,1,0:T(8,128)S(1)}) custom-call(f32[32,8,128]{2,1,0:T(8,128)S(1)} %copy-done.1, f32[96,256]{1,0:T(8,128)S(1)} %dynamic-slice_bitcast_fusion.1.refs_1_, f32[256,32]{1,0:T(8,128)S(1)} %dynamic-slice_bitcast_fusion.refs_2_), custom_call_target="tpu_custom_call" | custom-call | tf_op jit(solution)/shard_map/match/pallas_call | solution.py:440
  215.9 0.0 copy-start
  215.9 0.6 copy-done
  216.6 110.8 %residual.1 = bf16[128,2,2,64,128]{4,3,2,1,0:T(8,128)(2,1)} custom-call(bf16[32,2,2,64,512]{4,3,2,1,0:T(8,128)(2,1)} %get-tuple-element.8.refs_2_.refs_3_.refs_4_.refs_5_.x_ref, bf16[32,2,2,64,512]{4,3,2,1,0:T(8,128)(2,1)} %get-tuple-element.10.p_ref, f32[32,8,128]{2,1,0:T(8,128)} %copy-done), custom_call_target="tpu_custom_call" | custom-call | tf_op jit(solution)/shard_map/residual/pallas_call | solution.py:535
  327.3 13.1 %transform0.1 = bf16[64,128,512]{2,1,0:T(8,128)(2,1)} custom-call(bf16[512,64,128]{2,1,0:T(8,128)(2,1)} %bitcast.7, bf16[512,512]{1,0:T(8,128)(2,1)} %constant.22.clone.t_ref), custom_call_target="tpu_custom_call" | custom-call | flops 2000000000 | bytes 12000000 | tf_op jit(solution)/shard_map/transform0/pallas_call | solution.py:584
  340.4 0.7 copy.8
Async XLA Ops:
  181.5 0.9 copy-start.1
  215.9 0.7 copy-start

commit v2 on v0

v2 whole, which is shorter than its diff:
```python
import math

import jax
import jax.numpy as jnp
import numpy as np
from jax import lax
from jax.experimental import pallas as pl
from jax.experimental.pallas import tpu as pltpu
from jax.sharding import PartitionSpec as P

F = 256
TAPS = 31
STEPS = 3
HALF = (TAPS - 1) // 2
REG = 2.0
N_SHOT = 32
N_FREQ = 4
N_DEV = N_SHOT * N_FREQ
FL = F // N_DEV
SD = 64
R = 512
BLK = 16
MIB = 1 << 20
LIMIT = 60 * MIB
GROUP = 4
WINDOW = 8
HIGH = lax.Precision.HIGHEST
MESH = pl.DeviceIdType.MESH


def device_freqs():
    dev = np.arange(N_DEV)
    return (dev % N_FREQ)[:, None] * (F // N_FREQ) + (dev // N_FREQ)[:, None] * FL + np.arange(FL)[None, :]


def angle(freq, step):
    return ((freq * step) % (2 * F)).astype(np.float64) * (2.0 * math.pi / (2 * F))


def corr_table():
    freqs = device_freqs().reshape(N_SHOT, N_FREQ, FL)
    lags = np.abs(np.arange(64) - (TAPS - 1))
    taps = np.arange(32) - HALF
    table = np.zeros((N_FREQ, 96, N_SHOT, 8))
    for j in range(FL):
        col = freqs[:, :, j].T[:, None, :]
        table[:, :64, :, 3 * j] = np.cos(angle(col, lags[None, :, None]))
        table[:, 64:, :, 3 * j + 1] = np.cos(angle(col, taps[None, :, None]))
        table[:, 64:, :, 3 * j + 2] = -np.sin(angle(col, taps[None, :, None]))
    return table.reshape(N_FREQ, 96, N_SHOT * 8).astype(np.float32)


def resp_table():
    freqs = device_freqs().reshape(N_SHOT, N_FREQ, FL)
    taps = np.arange(32) - HALF
    valid = np.arange(32) < TAPS
    table = np.zeros((N_FREQ, N_SHOT, 8, 32))
    for j in range(FL):
        ang = angle(freqs[:, :, j].T[:, :, None], taps[None, None, :])
        table[:, :, j] = np.cos(ang) * valid
        table[:, :, FL + j] = -np.sin(ang) * valid
    return table.reshape(N_FREQ, N_SHOT * 8, 32).astype(np.float32)


def time_table():
    freqs = device_freqs()
    ang = angle(freqs[:, :, None], np.arange(2 * F)[None, None, :])
    norm = 1.0 / math.sqrt(F)
    table = np.stack([np.cos(ang) * norm, -np.sin(ang) * norm], axis=1)
    return table.reshape(2 * F, 2 * F).astype(np.float32)


def turned(back, offset, size):
    return jnp.where(back == 1, lax.rem(size - offset, size), offset)


def shot_at(me, d, back):
    x = lax.rem(me // 16 + d // 16, 2)
    z = lax.rem(lax.rem(me // 4, 4) + turned(back, lax.rem(d // 4, 4), 4), 4)
    y = lax.rem(lax.rem(me, 4) + turned(back, lax.rem(d, 4), 4), 4)
    return x * 16 + z * 4 + y


def shot_peer_of(me, me_freq, n):
    return shot_at(me, lax.rem(n * 19, N_SHOT), lax.rem(me_freq, 2))


def shot_source_of(me, me_freq, n):
    return shot_at(me, lax.rem(n * 19, N_SHOT), 1 - lax.rem(me_freq, 2))


def any_peer_of(me, me_freq, n):
    core = lax.rem(me_freq, 2)
    d = lax.rem(n * 43, N_DEV)
    x = lax.rem((me_freq // 2) * 2 + me // 16 + turned(core, lax.rem(d // 16, 4), 4), 4)
    z = lax.rem(lax.rem(me // 4, 4) + turned(core, lax.rem(d // 4, 4), 4), 4)
    y = lax.rem(lax.rem(me, 4) + turned(core, lax.rem(d, 4), 4), 4)
    other = lax.rem(core + d // 64, 2)
    return lax.rem(x, 2) * 16 + z * 4 + y, (x // 2) * 2 + other


def fused_kernel(
    damping, gain,
    owners_ref, rec_ref, shot_ref, ct_ref, rt_ref,
    out_ref, filt_ref,
    block, wide, narrow, coeffs, xb, cb, pb, w_ref, corr, arrived, parts, answer, resp_ref, ext_ref, sb,
    load_sem, own_sem, dsend, drecv, csend, crecv, qsend, qrecv, fsend, frecv, rsend, rrecv, send_sem, recv_sem,
):
    me = lax.axis_index("shot")
    me_freq = lax.axis_index("freq")
    mine = me * N_FREQ + me_freq
    freqs = rec_ref.shape[1]
    rows = 2 * freqs
    width = R // N_FREQ

    def remote(src, dst, send, recv, device):
        return pltpu.make_async_remote_copy(
            src_ref=src, dst_ref=dst, send_sem=send, recv_sem=recv, device_id=device, device_id_type=MESH
        )

    def data_copy(n):
        peer = shot_peer_of(me, me_freq, n)
        return remote(
            rec_ref.at[:, pl.ds(peer * FL, FL)], xb.at[me], dsend.at[n], drecv.at[n], (peer, me_freq)
        )

    def coeff_copy(n):
        peer = shot_peer_of(me, me_freq, n)
        return remote(
            coeffs.at[pl.ds(peer * FL, FL)], cb.at[me], csend.at[n], crecv.at[n], (peer, me_freq)
        )

    def corr_copy(n):
        peer = shot_source_of(me, me_freq, n)
        return remote(corr.at[peer], arrived.at[me], qsend.at[n], qrecv.at[n], (peer, me_freq))

    def part_copy(e):
        other = lax.rem(me_freq + e, N_FREQ)
        return remote(parts.at[me_freq], parts.at[me_freq], fsend.at[e], frecv.at[e], (me, other))

    def resp_copy(n):
        peer = shot_peer_of(me, me_freq, n)
        return remote(answer.at[peer], resp_ref.at[me], rsend.at[n], rrecv.at[n], (peer, me_freq))

    def residual_copy(n):
        return remote(
            sb.at[n], out_ref.at[mine], send_sem.at[n], recv_sem.at[n], any_peer_of(me, me_freq, n)
        )

    def run(first, last, action):
        def step(n, carry):
            action(n)
            return carry

        lax.fori_loop(first, last, step, 0)

    def load(b):
        return pltpu.make_async_copy(
            rec_ref.at[:, :, pl.ds(b * BLK, BLK), :], block.at[b % 2], load_sem.at[b % 2]
        )

    load(0).start()
    barrier = pltpu.get_barrier_semaphore()
    run(
        1,
        N_DEV,
        lambda n: pl.semaphore_signal(
            barrier, 1, device_id=any_peer_of(me, me_freq, n), device_id_type=MESH
        ),
    )
    pl.semaphore_wait(barrier, N_DEV - 1)

    def send_next(copy, n):
        copy(n - WINDOW).wait_send()
        copy(n).start()

    for n in range(1, WINDOW + 1):
        data_copy(n).start()
    own = pltpu.make_async_copy(rec_ref.at[:, pl.ds(me * FL, FL)], xb.at[me], own_sem.at[0])
    own.start()
    slot = lax.broadcasted_iota(jnp.int32, (4 * SD, R), 0)
    key = jnp.where(slot < SD, owners_ref[0] * SD + slot, owners_ref[1] * SD + slot - SD)
    key = jnp.where(slot < 2 * SD, key, owners_ref[2] * SD + slot - 2 * SD)
    key = jnp.where(slot < 3 * SD, key, -1)
    for b in range(SD // BLK):
        if b + 1 < SD // BLK:
            load(b + 1).start()
        load(b).wait()
        for ch in range(R // 128):
            part = block[b % 2, :, :, :, ch * 128 : (ch + 1) * 128]
            wide[ch] = part.astype(jnp.float32).reshape(rows * BLK, 128)

        def bin_shot(m, carry):
            data = jnp.concatenate(
                [wide[ch, pl.ds(m, rows, stride=BLK), :] for ch in range(R // 128)], axis=1
            ).astype(jnp.bfloat16)
            where = shot_ref[pl.ds(b * BLK + m, 1), :]
            one_hot = (jnp.broadcast_to(where, key.shape) == key).astype(jnp.bfloat16)
            out = lax.dot_general(
                data, one_hot, (((1,), (1,)), ((), ())), preferred_element_type=jnp.float32
            )
            real, imag = out[:freqs], out[freqs:]
            narrow[0, pl.ds(m, freqs, stride=BLK), :] = real[:, :128]
            narrow[1, pl.ds(m, freqs, stride=BLK), :] = real[:, 128:] + pltpu.roll(imag[:, 128:], SD, 1)
            narrow[2, pl.ds(m, freqs, stride=BLK), :] = imag[:, :128]
            due = b * BLK + m

            @pl.when((lax.rem(due, 2) == 0) & (due // 2 + WINDOW + 1 < N_SHOT))
            def _():
                send_next(data_copy, due // 2 + WINDOW + 1)

            return carry

        lax.fori_loop(0, BLK, bin_shot, 0)
        for ch in range(3):
            part = narrow[ch].reshape(freqs, BLK, 128).astype(jnp.bfloat16)
            coeffs[:, b * BLK : (b + 1) * BLK, ch * 128 : (ch + 1) * 128] = part
    kept = pltpu.make_async_copy(coeffs.at[pl.ds(me * FL, FL)], cb.at[me], own_sem.at[1])
    kept.start()

    def data_to_coeff(n):
        data_copy(N_SHOT - 1 - WINDOW + n).wait_send()
        coeff_copy(n).start()

    run(1, WINDOW + 1, data_to_coeff)
    run(WINDOW + 1, N_SHOT, lambda n: send_next(coeff_copy, n))
    own.wait()
    kept.wait()
    run(1, N_SHOT, lambda n: data_copy(n).wait_recv())

    for j in range(FL):
        for t in range(STEPS):
            owner = owners_ref[t]
            real, imag = xb[owner, 0, j], xb[owner, 1, j]
            under = 3 if t == 2 else 4 + t
            top = slice(t * SD, (t + 1) * SD)
            low = slice(under * SD, (under + 1) * SD)
            w_ref[j, top, :R] = real
            w_ref[j, top, R:] = imag
            w_ref[j, low, :R] = -imag
            w_ref[j, low, R:] = real

    lane = lax.broadcasted_iota(jnp.int32, (GROUP * SD, 128), 1)

    def predict_group(g, carry):
        for i in range(GROUP):
            if i == 0:

                @pl.when(g > 0)
                def _():
                    coeff_copy(g * GROUP).wait_recv()
            else:
                coeff_copy(g * GROUP + i).wait_recv()
        shots = [shot_source_of(me, me_freq, g * GROUP + i) for i in range(GROUP)]
        cols = jnp.zeros((GROUP * SD, 128), jnp.float32)
        for j in range(FL):
            lhs = jnp.concatenate([cb[s, j] for s in shots], axis=0)
            acc = jnp.dot(lhs, w_ref[j], preferred_element_type=jnp.float32)
            pred = (gain * acc).astype(jnp.bfloat16)
            pr, pi = pred[:, :R], pred[:, R:]
            for i, s in enumerate(shots):
                pb[s, 0, j] = pr[i * SD : (i + 1) * SD]
                pb[s, 1, j] = pi[i * SD : (i + 1) * SD]
            pr, pi = pr.astype(jnp.float32), pi.astype(jnp.float32)
            xr = jnp.concatenate([xb[s, 0, j] for s in shots], axis=0).astype(jnp.float32)
            xi = jnp.concatenate([xb[s, 1, j] for s in shots], axis=0).astype(jnp.float32)
            spec = jnp.sum(pr * pr + pi * pi, axis=1, keepdims=True)
            cr = jnp.sum(pr * xr + pi * xi, axis=1, keepdims=True)
            ci = jnp.sum(pr * xi - pi * xr, axis=1, keepdims=True)
            for q, col in enumerate((spec, cr, ci)):
                cols = jnp.where(lane == 3 * j + q, col, cols)
        flat = cols.T[:8]
        for i, s in enumerate(shots):
            pair = flat[:, (i // 2) * 128 : (i // 2) * 128 + 128]
            corr[s] = pair if i % 2 == 0 else pltpu.roll(pair, SD, 1)
        for i in range(GROUP):
            if i == 0:

                @pl.when(g > 0)
                def _():
                    corr_copy(g * GROUP).start()
            else:
                corr_copy(g * GROUP + i).start()
        return carry

    lax.fori_loop(0, N_SHOT // GROUP, predict_group, 0)
    arrived[me] = corr[me]
    run(1, N_SHOT, lambda n: corr_copy(n).wait_recv())

    parts[me_freq] = jnp.dot(
        ct_ref[...],
        arrived[...].reshape(N_SHOT * 8, 128),
        precision=HIGH,
        preferred_element_type=jnp.float32,
    )
    for e in range(1, N_FREQ):
        part_copy(e).start()
    for e in range(1, N_FREQ):
        part_copy(e).wait()
    total = parts[0]
    for e in range(1, N_FREQ):
        total = total + parts[e]
    row64 = lax.broadcasted_iota(jnp.int32, (64, 128), 0)
    row = lax.broadcasted_iota(jnp.int32, (32, 128), 0)
    ext_ref[...] = total[:64] + jnp.where(row64 == TAPS - 1, damping, 0.0)
    rhs = total[64:] + jnp.where(row == HALF, damping, 0.0)
    cols = [ext_ref[pl.ds(TAPS - 1 - k, 32), :] for k in range(TAPS)]
    inverse = []
    for p in range(TAPS):
        inv = 1.0 / cols[p][p : p + 1, :]
        inverse.append(inv)
        if p == TAPS - 1:
            break
        factor = jnp.where(row > p, cols[p] * inv, 0.0)
        rhs = rhs - factor * rhs[p : p + 1, :]
        for k in range(p + 1, TAPS):
            cols[k] = cols[k] - factor * cols[k][p : p + 1, :]
    found = jnp.zeros((32, 128), jnp.float32)
    for p in range(TAPS - 1, -1, -1):
        value = rhs[p : p + 1, :] * inverse[p]
        found = jnp.where(row == p, value, found)
        rhs = rhs - cols[p] * value
    resp = jnp.dot(rt_ref[...], found, precision=HIGH, preferred_element_type=jnp.float32)
    answer[...] = resp.reshape(N_SHOT, 8, 128)
    run(1, N_SHOT, lambda n: resp_copy(n).start())
    resp_ref[me] = answer[me]
    filt_ref[...] = jnp.concatenate([found, jnp.zeros((96, 128), jnp.float32)], axis=0).T[:SD]
    run(1, N_SHOT, lambda n: resp_copy(n).wait_recv())

    diagonal = lax.broadcasted_iota(jnp.int32, (SD, 128), 0) == lax.broadcasted_iota(
        jnp.int32, (SD, 128), 1
    )

    def compute(n):
        shot, freq = any_peer_of(me, me_freq, n)
        resp = resp_ref[shot]
        part = pl.ds(pl.multiple_of(freq * width, width), width)

        def column(q):
            spread = jnp.broadcast_to(resp[q : q + 1], (SD, 128))
            return jnp.sum(jnp.where(diagonal, spread, 0.0), axis=1, keepdims=True)

        for j in range(FL):
            real, imag = column(j), column(FL + j)
            xr = xb[shot, 0, j, :, part].astype(jnp.float32)
            xi = xb[shot, 1, j, :, part].astype(jnp.float32)
            pr = pb[shot, 0, j, :, part].astype(jnp.float32)
            pi = pb[shot, 1, j, :, part].astype(jnp.float32)
            sb[n, 0, j] = (xr - (real * pr - imag * pi)).astype(jnp.bfloat16)
            sb[n, 1, j] = (xi - (real * pi + imag * pr)).astype(jnp.bfloat16)

    def residual_step(n):
        compute(n)
        residual_copy(n).start()

    run(1, N_DEV, residual_step)
    compute(0)
    stay = pltpu.make_async_copy(sb.at[0], out_ref.at[mine], own_sem.at[2])
    stay.start()
    stay.wait()
    run(N_SHOT - WINDOW, N_SHOT, lambda n: coeff_copy(n).wait_send())
    run(1, N_SHOT, lambda n: corr_copy(n).wait_send())
    run(1, N_SHOT, lambda n: resp_copy(n).wait_send())
    run(1, N_DEV, lambda n: residual_copy(n).wait())


def fused(owners, recorded, rec_shot, ct, rt, damping, gain):
    freqs = recorded.shape[1]
    width = 2 * STEPS * SD
    anywhere = pl.BlockSpec(memory_space=pl.ANY)
    whole = pl.BlockSpec(memory_space=pltpu.VMEM)
    slab = (N_SHOT, 2, FL, SD, R)
    small = (N_SHOT, 8, 128)
    pairs = [N_SHOT, N_SHOT, N_SHOT, N_FREQ, N_SHOT, N_DEV]
    return pl.pallas_call(
        lambda *refs: fused_kernel(damping, gain, *refs),
        in_specs=[pl.BlockSpec(memory_space=pltpu.SMEM), anywhere, whole, whole, whole],
        out_specs=[anywhere, whole],
        out_shape=(
            jax.ShapeDtypeStruct((N_DEV, 2, FL, SD, R // N_FREQ), jnp.bfloat16),
            jax.ShapeDtypeStruct((SD, 128), jnp.float32),
        ),
        scratch_shapes=[
            pltpu.VMEM((2, 2, freqs, BLK, R), jnp.bfloat16),
            pltpu.VMEM((R // 128, 2 * freqs * BLK, 128), jnp.float32),
            pltpu.VMEM((3, freqs * BLK, 128), jnp.float32),
            pltpu.VMEM((freqs, SD, width), jnp.bfloat16),
            pltpu.VMEM(slab, jnp.bfloat16),
            pltpu.VMEM((N_SHOT, FL, SD, width), jnp.bfloat16),
            pltpu.VMEM(slab, jnp.bfloat16),
            pltpu.VMEM((FL, width, 2 * R), jnp.bfloat16),
            pltpu.VMEM(small, jnp.float32),
            pltpu.VMEM(small, jnp.float32),
            pltpu.VMEM((N_FREQ, 96, 128), jnp.float32),
            pltpu.VMEM(small, jnp.float32),
            pltpu.VMEM(small, jnp.float32),
            pltpu.VMEM((64, 128), jnp.float32),
            pltpu.VMEM((N_DEV, 2, FL, SD, R // N_FREQ), jnp.bfloat16),
            pltpu.SemaphoreType.DMA((2,)),
            pltpu.SemaphoreType.DMA((3,)),
        ]
        + [pltpu.SemaphoreType.DMA((count,)) for count in pairs for _ in range(2)],
        compiler_params=pltpu.CompilerParams(
            collective_id=0, has_side_effects=True, vmem_limit_bytes=LIMIT
        ),
        name="fused",
    )(owners, recorded, rec_shot, ct, rt)


def transform_kernel(r_ref, t_ref, *rest):
    out_ref, wide_ref = rest[-2:]
    k = r_ref.shape[0]
    s = r_ref.shape[1]
    wide_ref[...] = r_ref[...].astype(jnp.float32).reshape(k * s, 128)
    group = 4
    for m in range(0, s, group):
        rows = jnp.concatenate(
            [wide_ref[pl.ds(m + g, k, stride=s), :].T.astype(jnp.bfloat16) for g in range(group)], axis=0
        )
        out = jnp.dot(rows, t_ref[...], preferred_element_type=jnp.float32).astype(jnp.bfloat16)
        out_ref[m : m + group] = out.reshape(group, 128, 2 * F)


def transform(spectra, table, chunk, before):
    k, shots, recv = spectra.shape
    step = 16
    base = chunk * (shots // step)
    in_specs = [
        pl.BlockSpec((k, step, recv), lambda i: (0, i, 0)),
        pl.BlockSpec((k, 2 * F), lambda i: (0, 0)),
    ]
    args = [spectra, table]
    alias = {}
    if before is not None:
        in_specs.append(pl.BlockSpec(memory_space=pl.ANY))
        args.append(before)
        alias = {2: 0}
    return pl.pallas_call(
        transform_kernel,
        grid=(shots // step,),
        in_specs=in_specs,
        out_specs=pl.BlockSpec((step, recv, 2 * F), lambda i: (i + base, 0, 0)),
        out_shape=jax.ShapeDtypeStruct((SD, recv, 2 * F), jnp.bfloat16),
        scratch_shapes=[pltpu.VMEM((k * step, recv), jnp.float32)],
        input_output_aliases=alias,
        compiler_params=pltpu.CompilerParams(
            dimension_semantics=("arbitrary",), vmem_limit_bytes=LIMIT
        ),
        cost_estimate=pl.CostEstimate(flops=2 * 10**9, bytes_accessed=12 * 10**6, transcendentals=0),
        name=f"transform{chunk}",
    )(*args)


def per_device(recorded, rec_shot, owners):
    gain = (N_SHOT / (2.0 * R * STEPS)) ** 0.5
    me_freq = lax.axis_index("freq")
    ct = lax.dynamic_index_in_dim(jnp.asarray(corr_table()), me_freq, 0, False)
    rt = lax.dynamic_index_in_dim(jnp.asarray(resp_table()), me_freq, 0, False)
    table = jnp.asarray(time_table(), dtype=jnp.bfloat16)
    res, filt = fused(owners, recorded, rec_shot, ct, rt, REG * R * F, gain)
    primaries = transform(res.reshape(2 * F, SD, R // N_FREQ), table, 0, None)
    return (primaries, filt[:, :TAPS])


def solution(mesh):
    placed = (P(None, "freq", "shot", None), P("shot", None), P())
    return jax.shard_map(
        per_device,
        mesh=mesh,
        in_specs=placed,
        out_specs=(P("shot", "freq", None), P("shot", None)),
        check_vma=False,
    )
```

time: 1160 us -> 326 us (0.28); the launches traced: 1140 us -> 326 us
  waiting for transfers between devices: 602 us -> 0 us
  Pallas kernels: 0 us -> 322 us
  other arithmetic: 265 us -> 0 us
  local copies, waits for them, and re-layouts: 172 us -> 3.8 us
  matrix products: 63.8 us -> 0 us
  between operations: 18.6 us -> 0.65 us
  blocking collectives: 13.8 us -> 0 us
    psum x1 -> x0, waiting for transfers between devices: 511 us -> none  [broadcast(): return lax.psum(kept, axis)]
    pallas_call x0 -> x2, Pallas kernels: none -> 322 us  [the longest x1 309 us: fused(): pl.pallas_call(lambda *refs: fused_kernel(damping, gain, *refs), in_specs...]
    another operation x18 -> x0, other arithmetic: 225 us -> none  [the longest x4 182 us: solve_filters(): factor = jnp.linalg.cholesky(normal)]
    all_to_all x1 -> x0, waiting for transfers between devices: 91.6 us -> none  [per_device(): lax.all_to_all(residual, 'freq', split_axis=3, concat_axis=1, tiled=True)]
    unnamed x14 -> x3, local copies, waits for them, and re-layouts: 69.1 us -> 0.69 us
    dot_general x9 -> x0, matrix products: 53.3 us -> none  [the longest x3 41.3 us: product_step(): jnp.einsum('cfsk,fkr->cfsr', stacked, right_side, preferred_element_type=...]
    another operation x2 -> x0, local copies, waits for them, and re-layouts: 35 us -> none  [the longest x1 34.3 us: per_device(): residual = jnp.stack([res_real, res_imag]).astype(jnp.bfloat16)]
    all_to_all x1 -> x0, local copies, waits for them, and re-layouts: 34.3 us -> none  [per_device(): lax.all_to_all(residual, 'freq', split_axis=3, concat_axis=1, tiled=True)]
  transfers between devices with their start and end apart: 2 -> 0, of which waited for: 2 -> 0; matrix products, arithmetic and copies ran while one was open for 4% -> 0% of each run, Pallas kernels for 0% -> 0%
where the time goes in v2:
time: 326 us
  Pallas kernels  322 us (99%)
  local copies, waits for them, and re-layouts  3.8 us (1%)
    pallas_call x1, Pallas kernels, fused(): pl.pallas_call(lambda *refs: fused_kernel(damping, gain, *refs), in_specs...  309 us
    pallas_call x1, Pallas kernels, transform(): pl.pallas_call(transform_kernel, grid=(shots // step,), in_specs=in_specs...  13.1 us

profile of v2, /device:TPU:1, one launch (start us, length us, event | category | flops | bytes accessed | tf_op | source)
XLA Modules:
  0.0 326.1 jit_solution(15078732058065548936)
XLA Ops:
  0.6 1.5 dynamic-slice_bitcast_fusion.1.refs_3_
  2.2 1.6 dynamic-slice_bitcast_fusion.refs_4_
  3.7 308.6 %fused.1 = (bf16[128,2,2,64,128]{4,3,2,1,0:T(8,128)(2,1)}, f32[64,128]{1,0:T(8,128)}) custom-call(s32[3]{0:T(128)} %refs_0_.1, bf16[2,64,64,512]{3,2,1,0:T(8,128)(2,1)} %refs_1_.1, s32[64,512]{1,0:T(8,128)} %refs_2_.1, f32[96,256]{1,0:T(8,128)} %dynamic-slice_bitcast_fusion.1.refs_3_, f32[256,32]{1,0:T(8,128)} %dynamic-slice_bitcast_fusion.refs_4_), custom_call_target="tpu_custom_call" | custom-call | tf_op jit(solution)/shard_map/fused/pallas_call | solution.py:375
  312.3 0.0 copy-start
  312.3 13.1 %transform0.1 = bf16[64,128,512]{2,1,0:T(8,128)(2,1)} custom-call(bf16[512,64,128]{2,1,0:T(8,128)(2,1)} %bitcast.6, bf16[512,512]{1,0:T(8,128)(2,1)} %constant.22.clone.t_ref), custom_call_target="tpu_custom_call" | custom-call | flops 2000000000 | bytes 12000000 | tf_op jit(solution)/shard_map/transform0/pallas_call | solution.py:438
  325.4 0.0 copy-done
  325.4 0.7 copy.8
Async XLA Ops:
  312.3 13.1 %copy-start = (f32[64,128]{1,0:T(8,128)S(1)}, f32[64,128]{1,0:T(8,128)}, u32[]{:S(2)}) copy-start(f32[64,128]{1,0:T(8,128)} %get-tuple-element.5) | copy-start | bytes 98308

commit v3 on v2

--- a/solution.py
+++ b/solution.py
@@ -23,6 +23,7 @@
 MIB = 1 << 20
 LIMIT = 60 * MIB
 GROUP = 4
+AHEAD = 16
 WINDOW = 8
 HIGH = lax.Precision.HIGHEST
 MESH = pl.DeviceIdType.MESH
@@ -101,9 +102,9 @@
 
 def fused_kernel(
     damping, gain,
-    owners_ref, rec_ref, shot_ref, ct_ref, rt_ref,
+    owners_ref, rec_ref, shot_ref, cts_ref, rts_ref,
     out_ref, filt_ref,
-    block, wide, narrow, coeffs, xb, cb, pb, w_ref, corr, arrived, parts, answer, resp_ref, ext_ref, sb,
+    block, wide, narrow, coeffs, xb, cb, pb, w_ref, corr, arrived, parts, answer, resp_ref, ext_ref, sb, ct_ref, rt_ref,
     load_sem, own_sem, dsend, drecv, csend, crecv, qsend, qrecv, fsend, frecv, rsend, rrecv, send_sem, recv_sem,
 ):
     me = lax.axis_index("shot")
@@ -159,16 +160,27 @@
             rec_ref.at[:, :, pl.ds(b * BLK, BLK), :], block.at[b % 2], load_sem.at[b % 2]
         )
 
+    tables = (
+        pltpu.make_async_copy(cts_ref.at[me_freq], ct_ref, own_sem.at[3]),
+        pltpu.make_async_copy(rts_ref.at[me_freq], rt_ref, own_sem.at[4]),
+    )
+
     load(0).start()
+    for table in tables:
+        table.start()
     barrier = pltpu.get_barrier_semaphore()
     run(
         1,
-        N_DEV,
+        N_SHOT,
         lambda n: pl.semaphore_signal(
-            barrier, 1, device_id=any_peer_of(me, me_freq, n), device_id_type=MESH
+            barrier, 1, device_id=(shot_peer_of(me, me_freq, n), me_freq), device_id_type=MESH
         ),
     )
-    pl.semaphore_wait(barrier, N_DEV - 1)
+    for e in range(1, N_FREQ):
+        pl.semaphore_signal(
+            barrier, 1, device_id=(me, lax.rem(me_freq + e, N_FREQ)), device_id_type=MESH
+        )
+    pl.semaphore_wait(barrier, N_SHOT + N_FREQ - 2)
 
     def send_next(copy, n):
         copy(n - WINDOW).wait_send()
@@ -223,7 +235,7 @@
         coeff_copy(n).start()
 
     run(1, WINDOW + 1, data_to_coeff)
-    run(WINDOW + 1, N_SHOT, lambda n: send_next(coeff_copy, n))
+    run(WINDOW + 1, AHEAD, lambda n: coeff_copy(n).start())
     own.wait()
     kept.wait()
     run(1, N_SHOT, lambda n: data_copy(n).wait_recv())
@@ -251,6 +263,12 @@
                     coeff_copy(g * GROUP).wait_recv()
             else:
                 coeff_copy(g * GROUP + i).wait_recv()
+
+        @pl.when(AHEAD + g * GROUP < N_SHOT)
+        def _():
+            for i in range(GROUP):
+                coeff_copy(AHEAD + g * GROUP + i).start()
+
         shots = [shot_source_of(me, me_freq, g * GROUP + i) for i in range(GROUP)]
         cols = jnp.zeros((GROUP * SD, 128), jnp.float32)
         for j in range(FL):
@@ -287,6 +305,8 @@
     arrived[me] = corr[me]
     run(1, N_SHOT, lambda n: corr_copy(n).wait_recv())
 
+    for table in tables:
+        table.wait()
     parts[me_freq] = jnp.dot(
         ct_ref[...],
         arrived[...].reshape(N_SHOT * 8, 128),
@@ -358,7 +378,7 @@
     stay = pltpu.make_async_copy(sb.at[0], out_ref.at[mine], own_sem.at[2])
     stay.start()
     stay.wait()
-    run(N_SHOT - WINDOW, N_SHOT, lambda n: coeff_copy(n).wait_send())
+    run(1, N_SHOT, lambda n: coeff_copy(n).wait_send())
     run(1, N_SHOT, lambda n: corr_copy(n).wait_send())
     run(1, N_SHOT, lambda n: resp_copy(n).wait_send())
     run(1, N_DEV, lambda n: residual_copy(n).wait())
@@ -374,7 +394,7 @@
     pairs = [N_SHOT, N_SHOT, N_SHOT, N_FREQ, N_SHOT, N_DEV]
     return pl.pallas_call(
         lambda *refs: fused_kernel(damping, gain, *refs),
-        in_specs=[pl.BlockSpec(memory_space=pltpu.SMEM), anywhere, whole, whole, whole],
+        in_specs=[pl.BlockSpec(memory_space=pltpu.SMEM), anywhere, whole, anywhere, anywhere],
         out_specs=[anywhere, whole],
         out_shape=(
             jax.ShapeDtypeStruct((N_DEV, 2, FL, SD, R // N_FREQ), jnp.bfloat16),
@@ -396,8 +416,10 @@
             pltpu.VMEM(small, jnp.float32),
             pltpu.VMEM((64, 128), jnp.float32),
             pltpu.VMEM((N_DEV, 2, FL, SD, R // N_FREQ), jnp.bfloat16),
+            pltpu.VMEM(ct.shape[1:], jnp.float32),
+            pltpu.VMEM(rt.shape[1:], jnp.float32),
             pltpu.SemaphoreType.DMA((2,)),
-            pltpu.SemaphoreType.DMA((3,)),
+            pltpu.SemaphoreType.DMA((5,)),
         ]
         + [pltpu.SemaphoreType.DMA((count,)) for count in pairs for _ in range(2)],
         compiler_params=pltpu.CompilerParams(
@@ -453,9 +475,7 @@
 
 def per_device(recorded, rec_shot, owners):
     gain = (N_SHOT / (2.0 * R * STEPS)) ** 0.5
-    me_freq = lax.axis_index("freq")
-    ct = lax.dynamic_index_in_dim(jnp.asarray(corr_table()), me_freq, 0, False)
-    rt = lax.dynamic_index_in_dim(jnp.asarray(resp_table()), me_freq, 0, False)
+    ct, rt = jnp.asarray(corr_table()), jnp.asarray(resp_table())
     table = jnp.asarray(time_table(), dtype=jnp.bfloat16)
     res, filt = fused(owners, recorded, rec_shot, ct, rt, REG * R * F, gain)
     primaries = transform(res.reshape(2 * F, SD, R // N_FREQ), table, 0, None)

time: 326 us -> 314 us (0.963)
  Pallas kernels: 322 us -> 313 us
    pallas_call x1, Pallas kernels: 309 us -> 300 us  [fused(): pl.pallas_call(lambda *refs: fused_kernel(damping, gain, *refs), in_specs...]
where the time goes in v3:
time: 314 us
  Pallas kernels  313 us (100%)
    pallas_call x1, Pallas kernels, fused(): pl.pallas_call(lambda *refs: fused_kernel(damping, gain, *refs), in_specs...  300 us
    pallas_call x1, Pallas kernels, transform(): pl.pallas_call(transform_kernel, grid=(shots // step,), in_specs=in_specs...  13.1 us

profile of v3, /device:TPU:1, one launch (start us, length us, event | category | flops | bytes accessed | tf_op | source)
XLA Modules:
  0.0 313.9 jit_solution(1644057222329741863)
XLA Ops:
  0.6 299.5 %fused.1 = (bf16[128,2,2,64,128]{4,3,2,1,0:T(8,128)(2,1)}, f32[64,128]{1,0:T(8,128)}) custom-call(s32[3]{0:T(128)} %refs_0_.1, bf16[2,64,64,512]{3,2,1,0:T(8,128)(2,1)} %refs_1_.1, s32[64,512]{1,0:T(8,128)} %refs_2_.1, f32[4,96,256]{2,1,0:T(8,128)} %constant.6.clone.refs_3_, f32[4,256,32]{2,1,0:T(8,128)} %constant.7.clone.refs_4_), custom_call_target="tpu_custom_call" | custom-call | tf_op jit(solution)/shard_map/fused/pallas_call | solution.py:395
  300.1 0.0 copy-start
  300.2 13.1 %transform0.1 = bf16[64,128,512]{2,1,0:T(8,128)(2,1)} custom-call(bf16[512,64,128]{2,1,0:T(8,128)(2,1)} %bitcast.2, bf16[512,512]{1,0:T(8,128)(2,1)} %constant.8.clone.t_ref), custom_call_target="tpu_custom_call" | custom-call | flops 2000000000 | bytes 12000000 | tf_op jit(solution)/shard_map/transform0/pallas_call | solution.py:460
  313.2 0.0 copy-done
  313.2 0.7 copy.8
Async XLA Ops:
  300.1 13.1 %copy-start = (f32[64,128]{1,0:T(8,128)S(1)}, f32[64,128]{1,0:T(8,128)}, u32[]{:S(2)}) copy-start(f32[64,128]{1,0:T(8,128)} %get-tuple-element.5) | copy-start | bytes 98308

commit v4 on v3

--- a/solution.py
+++ b/solution.py
@@ -24,7 +24,7 @@
 LIMIT = 60 * MIB
 GROUP = 4
 AHEAD = 16
-WINDOW = 8
+WINDOW = 12
 HIGH = lax.Precision.HIGHEST
 MESH = pl.DeviceIdType.MESH
 
@@ -83,11 +83,11 @@
 
 
 def shot_peer_of(me, me_freq, n):
-    return shot_at(me, lax.rem(n * 19, N_SHOT), lax.rem(me_freq, 2))
+    return shot_at(me, lax.rem(n * 11, N_SHOT), lax.rem(me_freq, 2))
 
 
 def shot_source_of(me, me_freq, n):
-    return shot_at(me, lax.rem(n * 19, N_SHOT), 1 - lax.rem(me_freq, 2))
+    return shot_at(me, lax.rem(n * 11, N_SHOT), 1 - lax.rem(me_freq, 2))
 
 
 def any_peer_of(me, me_freq, n):
@@ -434,7 +434,7 @@
     k = r_ref.shape[0]
     s = r_ref.shape[1]
     wide_ref[...] = r_ref[...].astype(jnp.float32).reshape(k * s, 128)
-    group = 4
+    group = 8
     for m in range(0, s, group):
         rows = jnp.concatenate(
             [wide_ref[pl.ds(m + g, k, stride=s), :].T.astype(jnp.bfloat16) for g in range(group)], axis=0
@@ -445,7 +445,7 @@
 
 def transform(spectra, table, chunk, before):
     k, shots, recv = spectra.shape
-    step = 16
+    step = 8
     base = chunk * (shots // step)
     in_specs = [
         pl.BlockSpec((k, step, recv), lambda i: (0, i, 0)),

time: 314 us -> 302 us (0.962)
  Pallas kernels: 313 us -> 298 us
    pallas_call x1, Pallas kernels: 300 us -> 286 us  [fused(): pl.pallas_call(lambda *refs: fused_kernel(damping, gain, *refs), in_specs...]
where the time goes in v4:
time: 302 us; the launch traced here: 299 us
  Pallas kernels  298 us (99%)
    pallas_call x1, Pallas kernels, fused(): pl.pallas_call(lambda *refs: fused_kernel(damping, gain, *refs), in_specs...  286 us
    pallas_call x1, Pallas kernels, transform(): pl.pallas_call(transform_kernel, grid=(shots // step,), in_specs=in_specs...  11.8 us

profile of v4, /device:TPU:1, one launch (start us, length us, event | category | flops | bytes accessed | tf_op | source)
XLA Modules:
  0.0 299.3 jit_solution(10916367562634438754)
XLA Ops:
  0.6 286.2 %fused.1 = (bf16[128,2,2,64,128]{4,3,2,1,0:T(8,128)(2,1)}, f32[64,128]{1,0:T(8,128)}) custom-call(s32[3]{0:T(128)} %refs_0_.1, bf16[2,64,64,512]{3,2,1,0:T(8,128)(2,1)} %refs_1_.1, s32[64,512]{1,0:T(8,128)} %refs_2_.1, f32[4,96,256]{2,1,0:T(8,128)} %constant.6.clone.refs_3_, f32[4,256,32]{2,1,0:T(8,128)} %constant.7.clone.refs_4_), custom_call_target="tpu_custom_call" | custom-call | tf_op jit(solution)/shard_map/fused/pallas_call | solution.py:395
  286.8 0.0 copy-start
  286.8 11.8 %transform0.1 = bf16[64,128,512]{2,1,0:T(8,128)(2,1)} custom-call(bf16[512,64,128]{2,1,0:T(8,128)(2,1)} %bitcast.2, bf16[512,512]{1,0:T(8,128)(2,1)} %constant.8.clone.t_ref), custom_call_target="tpu_custom_call" | custom-call | flops 2000000000 | bytes 12000000 | tf_op jit(solution)/shard_map/transform0/pallas_call | solution.py:460
  298.6 0.0 copy-done
  298.6 0.7 copy.8
Async XLA Ops:
  286.8 11.8 %copy-start = (f32[64,128]{1,0:T(8,128)S(1)}, f32[64,128]{1,0:T(8,128)}, u32[]{:S(2)}) copy-start(f32[64,128]{1,0:T(8,128)} %get-tuple-element.5) | copy-start | bytes 98308

commit v5 on v4

--- a/solution.py
+++ b/solution.py
@@ -23,7 +23,7 @@
 MIB = 1 << 20
 LIMIT = 60 * MIB
 GROUP = 4
-AHEAD = 16
+AHEAD = 24
 WINDOW = 12
 HIGH = lax.Precision.HIGHEST
 MESH = pl.DeviceIdType.MESH

time: 302 us -> 300 us (level)
  no operation moved by 1% of the time
where the time goes in v5:
time: 300 us
  Pallas kernels  298 us (99%)
    pallas_call x1, Pallas kernels, fused(): pl.pallas_call(lambda *refs: fused_kernel(damping, gain, *refs), in_specs...  287 us
    pallas_call x1, Pallas kernels, transform(): pl.pallas_call(transform_kernel, grid=(shots // step,), in_specs=in_specs...  11.8 us

profile of v5, /device:TPU:1, one launch (start us, length us, event | category | flops | bytes accessed | tf_op | source)
XLA Modules:
  0.0 299.8 jit_solution(12787296137862916971)
XLA Ops:
  0.6 286.7 %fused.1 = (bf16[128,2,2,64,128]{4,3,2,1,0:T(8,128)(2,1)}, f32[64,128]{1,0:T(8,128)}) custom-call(s32[3]{0:T(128)} %refs_0_.1, bf16[2,64,64,512]{3,2,1,0:T(8,128)(2,1)} %refs_1_.1, s32[64,512]{1,0:T(8,128)} %refs_2_.1, f32[4,96,256]{2,1,0:T(8,128)} %constant.6.clone.refs_3_, f32[4,256,32]{2,1,0:T(8,128)} %constant.7.clone.refs_4_), custom_call_target="tpu_custom_call" | custom-call | tf_op jit(solution)/shard_map/fused/pallas_call | solution.py:395
  287.4 0.0 copy-start
  287.4 11.8 %transform0.1 = bf16[64,128,512]{2,1,0:T(8,128)(2,1)} custom-call(bf16[512,64,128]{2,1,0:T(8,128)(2,1)} %bitcast.2, bf16[512,512]{1,0:T(8,128)(2,1)} %constant.8.clone.t_ref), custom_call_target="tpu_custom_call" | custom-call | flops 2000000000 | bytes 12000000 | tf_op jit(solution)/shard_map/transform0/pallas_call | solution.py:460
  299.1 0.0 copy-done
  299.1 0.7 copy.8
Async XLA Ops:
  287.4 11.8 %copy-start = (f32[64,128]{1,0:T(8,128)S(1)}, f32[64,128]{1,0:T(8,128)}, u32[]{:S(2)}) copy-start(f32[64,128]{1,0:T(8,128)} %get-tuple-element.5) | copy-start | bytes 98308
